TPU v7x, 128 devices: a whole 4x4x4 slice. The times are simulated.
128 devices in a mesh: col: 32 (over z, y, x_hi), row: 4 (over x_lo, core).
Axes of the slice: x: 4 (x_hi: 2, x_lo: 2; x = x_hi * 2 + x_lo), y: 4, z: 4, core: 2. Of those that a mesh axis runs over, the one named last changes fastest.
Arguments:
- hamiltonian: float32 [16384, 16384], P('row', 'col'), as said below
Outputs:
- reduced: float32 [16384, 16384], P('row', 'col')
Inputs may be any that keep to these rules, and one draw needn't show every extreme that they name: hamiltonian is symmetric.
All inputs are finite; a program needn't handle non-finite values.
Results may differ from a plain program's by a relative error of at most 0.00019.
Values sent between devices are 32-bit elements; how exact they have to be, the bound alone decides.
No kernel may reach another device: no remote copies, remote signals or barrier semaphores. Data moves between devices by JAX's collectives and lax.ppermute only.
A program may use at most 128 MiB of HBM per device.

v0:
```python
import jax
import jax.numpy as jnp
from jax import lax
from jax.sharding import PartitionSpec as P

NB = 256
PANELS = 2


def from_root(block, axis, holder):
    block = jnp.where(lax.axis_index(axis) == holder, block, jnp.zeros_like(block))
    return lax.psum(block, axis)


def product(left, right):
    return jnp.dot(left, right, precision=lax.Precision.HIGHEST, preferred_element_type=jnp.float32)


def inner_tn(left, right):
    return lax.dot_general(
        left,
        right,
        (((0,), (0,)), ((), ())),
        precision=lax.Precision.HIGHEST,
        preferred_element_type=jnp.float32,
    )


def outer_nt(left, right):
    return lax.dot_general(
        left,
        right,
        (((1,), (1,)), ((), ())),
        precision=lax.Precision.HIGHEST,
        preferred_element_type=jnp.float32,
    )


def solve_right(gram, panel):
    lower = jnp.linalg.cholesky(gram)
    return lax.linalg.triangular_solve(lower, panel, left_side=False, lower=True, transpose_a=True)


def coupling_of(top_rows):
    square = jnp.eye(NB, dtype=jnp.float32) - top_rows.T
    normal_eq = inner_tn(square, square)
    factor = jnp.linalg.cholesky(normal_eq)
    middle = lax.linalg.triangular_solve(factor, square.T, left_side=True, lower=True)
    return lax.linalg.triangular_solve(factor, middle, left_side=True, lower=True, transpose_a=True)


def shards(hamiltonian):
    matrix = hamiltonian
    row_block = matrix.shape[0]
    col_block = matrix.shape[1]
    ratio = lax.axis_size("col") // lax.axis_size("row")
    row_pos = lax.axis_index("row")
    col_pos = lax.axis_index("col")
    global_rows = row_pos * row_block + jnp.arange(row_block, dtype=jnp.int32)
    owner = col_pos // ratio
    offset = col_pos % ratio * col_block
    for panel_index in range(PANELS):
        first_col = panel_index * NB
        first_row = first_col + NB
        live = (global_rows >= first_row)[:, None]
        panel = jnp.where(live, matrix[:, first_col : first_col + NB], jnp.float32(0.0))
        gram = lax.psum(inner_tn(panel, panel), "row")
        basis = solve_right(gram, panel)
        top_rows = from_root(basis[first_row : first_row + NB], "row", 0)
        coupling = coupling_of(top_rows)
        ident = (
            global_rows[:, None] - first_row == jnp.arange(NB, dtype=jnp.int32)[None, :]
        ).astype(jnp.float32)
        vectors = ident - basis
        vectors, coupling = (from_root(vectors, "col", 0), from_root(coupling, "col", 0))
        column_vectors = from_root(
            lax.dynamic_slice_in_dim(vectors, offset, col_block, 0), "row", owner
        )
        applied = lax.psum(product(matrix, column_vectors), "col")
        applied = product(applied, coupling)
        inner = lax.psum(inner_tn(vectors, applied), "row")
        inner = product(coupling.T, inner)
        shifted = applied - 0.5 * product(vectors, inner)
        column_shifted = from_root(
            lax.dynamic_slice_in_dim(shifted, offset, col_block, 0), "row", owner
        )
        matrix = matrix - outer_nt(vectors, column_shifted) - outer_nt(shifted, column_vectors)
    return matrix


def solution(mesh):
    return jax.shard_map(
        shards,
        mesh=mesh,
        in_specs=(P("row", "col"),),
        out_specs=P("row", "col"),
        check_vma=False,
    )
```

profile of v0, /device:TPU:1, one launch (start us, length us, event | category | flops | bytes accessed | tf_op | source)
XLA Modules:
  0.0 2289.1 jit_solution(8985189598274994049)
XLA Ops:
  24.4 39.6 %all-reduce.18.cloned.1.call-done = f32[256,256]{0,1:T(8,128)} async-done(((f32[256,256]{0,1:T(8,128)}), f32[256,256]{0,1:T(8,128)}) %all-reduce.18.cloned.1.call-update) | async-done | bytes 262160 | tf_op jit(solution)/shard_map/psum | solution.py:67
  66.1 11.7 cholesky.214
  77.8 9.8 custom-call.23
  88.2 11.7 cholesky.231
  106.4 19.7 custom-call.24
  139.4 357.7 %all-reduce.20.cloned.1.call-done = f32[4096,256]{0,1:T(8,128)} async-done(((f32[4096,256]{0,1:T(8,128)}), f32[4096,256]{0,1:T(8,128)}) %all-reduce.20.cloned.1.call-update) | async-done | bytes 4194320 | tf_op jit(solution)/shard_map/psum | solution.py:12
  499.5 60.5 %all-reduce.40.cloned.1.call-done = (f32[512,256]{0,1:T(8,128)}, f32[256,256]{0,1:T(8,128)}) async-done(((f32[512,256]{0,1:T(8,128)}, f32[256,256]{0,1:T(8,128)}), (f32[512,256]{0,1:T(8,128)}, f32[256,256]{0,1:T(8,128)})) %all-reduce.40.cloned.1.call-update) | async-done | bytes 786448 | tf_op jit(solution)/shard_map/psum | solution.py:12
  562.9 11.7 cholesky.248
  574.7 9.8 custom-call.25
  585.0 11.7 cholesky.265
  603.5 19.7 custom-call.27
  625.4 10.9 convolution_bitcast_fusion
  637.0 362.5 %all-reduce.36.cloned.1.call-done = (f32[4096,256]{0,1:T(8,128)}, f32[256,256]{0,1:T(8,128)}) async-done(((f32[4096,256]{0,1:T(8,128)}, f32[256,256]{0,1:T(8,128)}), (f32[4096,256]{0,1:T(8,128)}, f32[256,256]{0,1:T(8,128)})) %all-reduce.36.cloned.1.call-update) | async-done | bytes 4456464 | tf_op jit(solution)/shard_map/psum | solution.py:79
  1020.5 50.7 %all-reduce.22.cloned.1.call-done = f32[256,256]{1,0:T(8,128)} async-done(((f32[256,256]{1,0:T(8,128)}), f32[256,256]{1,0:T(8,128)}) %all-reduce.22.cloned.1.call-update) | async-done | bytes 262160 | tf_op jit(solution)/shard_map/psum | solution.py:81
  1083.5 38.6 %all-reduce.24.cloned.1.call-done = f32[512,256]{0,1:T(8,128)} async-done(((f32[512,256]{0,1:T(8,128)}), f32[512,256]{0,1:T(8,128)}) %all-reduce.24.cloned.1.call-update) | async-done | bytes 524304 | tf_op jit(solution)/shard_map/psum | solution.py:12
  1122.2 10.1 fusion.64
  1132.2 11.0 subtract_subtract_fusion.1
  1153.1 36.9 %all-reduce.26.cloned.1.call-done = f32[256,256]{0,1:T(8,128)} async-done(((f32[256,256]{0,1:T(8,128)}), f32[256,256]{0,1:T(8,128)}) %all-reduce.26.cloned.1.call-update) | async-done | bytes 262160 | tf_op jit(solution)/shard_map/psum | solution.py:67
  1192.1 11.7 cholesky.282
  1203.8 9.8 custom-call.28
  1214.1 11.7 cholesky.299
  1232.9 19.7 custom-call.29
  1265.9 357.7 %all-reduce.28.cloned.1.call-done = f32[4096,256]{0,1:T(8,128)} async-done(((f32[4096,256]{0,1:T(8,128)}), f32[4096,256]{0,1:T(8,128)}) %all-reduce.28.cloned.1.call-update) | async-done | bytes 4194320 | tf_op jit(solution)/shard_map/psum | solution.py:12
  1626.1 60.3 %all-reduce.38.cloned.1.call-done = (f32[512,256]{0,1:T(8,128)}, f32[256,256]{0,1:T(8,128)}) async-done(((f32[512,256]{0,1:T(8,128)}, f32[256,256]{0,1:T(8,128)}), (f32[512,256]{0,1:T(8,128)}, f32[256,256]{0,1:T(8,128)})) %all-reduce.38.cloned.1.call-update) | async-done | bytes 786448 | tf_op jit(solution)/shard_map/psum | solution.py:12
  1689.2 11.7 cholesky.316
  1711.3 11.7 cholesky.333
  1730.2 19.7 custom-call.32
  1752.0 16.9 fusion.66
  1769.7 362.3 %all-reduce.34.cloned.1.call-done = (f32[4096,256]{1,0:T(8,128)}, f32[256,256]{0,1:T(8,128)}) async-done(((f32[4096,256]{1,0:T(8,128)}, f32[256,256]{0,1:T(8,128)}), (f32[4096,256]{1,0:T(8,128)}, f32[256,256]{0,1:T(8,128)})) %all-reduce.34.cloned.1.call-update) | async-done | bytes 4456464 | tf_op jit(solution)/shard_map/psum | solution.py:79
  2149.8 50.4 %all-reduce.30.cloned.1.call-done = f32[256,256]{1,0:T(8,128)} async-done(((f32[256,256]{1,0:T(8,128)}), f32[256,256]{1,0:T(8,128)}) %all-reduce.30.cloned.1.call-update) | async-done | bytes 262160 | tf_op jit(solution)/shard_map/psum | solution.py:81
  2212.4 38.7 %all-reduce.32.cloned.1.call-done = f32[512,256]{0,1:T(8,128)} async-done(((f32[512,256]{0,1:T(8,128)}), f32[512,256]{0,1:T(8,128)}) %all-reduce.32.cloned.1.call-update) | async-done | bytes 524304 | tf_op jit(solution)/shard_map/psum | solution.py:12
  2260.7 12.4 subtract_subtract_fusion
  (195 shorter events, 206.3 us)
Async XLA Ops:
  6.5 57.5 %all-reduce.18.cloned.1.call-start = ((), (), s32[]{:S(2)}) async-start(), calls=%async_computation | async-start | bytes 524288 | tf_op jit(solution)/shard_map/psum | solution.py:67
  18.0 1.9 copy-start.1
  24.1 473.0 %all-reduce.20.cloned.1.call-start = ((), (), s32[]{:S(2)}) async-start(), calls=%async_computation.1 | async-start | bytes 8388608 | tf_op jit(solution)/shard_map/psum | solution.py:12
  126.0 3.7 copy-start.2
  133.7 1.4 copy-start.13
  137.6 422.4 %all-reduce.40.cloned.1.call-start = ((), (), s32[]{:S(2)}) async-start(), calls=%async_computation.11 | async-start | bytes 1572864 | tf_op jit(solution)/shard_map/psum | solution.py:12
  499.1 500.5 %all-reduce.36.cloned.1.call-start = ((), (), s32[]{:S(2)}) async-start(), calls=%async_computation.9 | async-start | bytes 8912896 | tf_op jit(solution)/shard_map/psum | solution.py:79
  560.0 65.3 %copy-start.16 = (f32[512,256]{0,1:T(8,128)S(1)}, f32[512,256]{0,1:T(8,128)}, u32[]{:S(2)}) copy-start(f32[512,256]{0,1:T(8,128)} %get-tuple-element.95) | copy-start | bytes 1572868
  637.0 434.2 %all-reduce.22.cloned.1.call-start = ((), (), s32[]{:S(2)}) async-start(), calls=%async_computation.2 | async-start | bytes 524288 | tf_op jit(solution)/shard_map/psum | solution.py:81
  999.5 10.8 copy-start.5
  1008.4 2.0 copy-start.7
  1014.7 56.5 %copy-start.17 = (f32[256,256]{0,1:T(8,128)S(1)}, f32[256,256]{0,1:T(8,128)}, u32[]{:S(2)}) copy-start(f32[256,256]{0,1:T(8,128)} %get-tuple-element.92) | copy-start | bytes 786436
  1014.7 107.5 %all-reduce.24.cloned.1.call-start = ((), (), s32[]{:S(2)}) async-start(), calls=%async_computation.3 | async-start | bytes 1048576 | tf_op jit(solution)/shard_map/psum | solution.py:12
  1080.6 2.0 copy-start.9
  1083.5 106.5 %all-reduce.26.cloned.1.call-start = ((), (), s32[]{:S(2)}) async-start(), calls=%async_computation.4 | async-start | bytes 524288 | tf_op jit(solution)/shard_map/psum | solution.py:67
  1122.2 10.1 copy-start.10
  1143.3 3.4 copy-start
  1146.7 1.9 copy-start.3
  1152.9 470.8 %all-reduce.28.cloned.1.call-start = ((), (), s32[]{:S(2)}) async-start(), calls=%async_computation.5 | async-start | bytes 8388608 | tf_op jit(solution)/shard_map/psum | solution.py:12
  1252.6 3.7 copy-start.4
  1260.3 1.4 copy-start.14
  1264.2 422.2 %all-reduce.38.cloned.1.call-start = ((), (), s32[]{:S(2)}) async-start(), calls=%async_computation.10 | async-start | bytes 1572864 | tf_op jit(solution)/shard_map/psum | solution.py:12
  1625.6 506.5 %all-reduce.34.cloned.1.call-start = ((), (), s32[]{:S(2)}) async-start(), calls=%async_computation.8 | async-start | bytes 8912896 | tf_op jit(solution)/shard_map/psum | solution.py:79
  1686.4 65.6 %copy-start.15 = (f32[512,256]{0,1:T(8,128)S(1)}, f32[512,256]{0,1:T(8,128)}, u32[]{:S(2)}) copy-start(f32[512,256]{0,1:T(8,128)} %get-tuple-element.93) | copy-start | bytes 1572868
  1769.6 430.5 %all-reduce.30.cloned.1.call-start = ((), (), s32[]{:S(2)}) async-start(), calls=%async_computation.6 | async-start | bytes 524288 | tf_op jit(solution)/shard_map/psum | solution.py:81
  2132.0 7.4 copy-start.6
  2137.5 2.0 copy-start.8
  2143.8 56.3 %copy-start.18 = (f32[256,256]{0,1:T(8,128)S(1)}, f32[256,256]{0,1:T(8,128)}, u32[]{:S(2)}) copy-start(f32[256,256]{0,1:T(8,128)} %get-tuple-element.90) | copy-start | bytes 786436
  2143.8 107.3 %all-reduce.32.cloned.1.call-start = ((), (), s32[]{:S(2)}) async-start(), calls=%async_computation.7 | async-start | bytes 1048576 | tf_op jit(solution)/shard_map/psum | solution.py:12
  2209.5 2.0 copy-start.11
  2251.1 9.6 copy-start.12
Sparse Core Ops, SparseCore 0:
  24.3 39.6 all-reduce.17
  137.8 359.3 all-reduce.19
  499.9 60.0 all-reduce.39
  637.1 362.3 all-reduce.35
  1014.8 56.3 all-reduce.21
  1083.6 38.5 all-reduce.23
  1153.0 36.9 all-reduce.25
  1264.3 359.2 all-reduce.27
  1626.2 60.0 all-reduce.37
  1769.8 362.2 all-reduce.33
  2143.9 56.1 all-reduce.29
  2212.5 38.5 all-reduce.31
where the time goes:
time: 2290 us
  waiting for transfers between devices  1820 us (79%)
  other arithmetic  239 us (10%)
  matrix products  145 us (6%)
  local copies, waits for them, and re-layouts  65.9 us (3%)
    psum x6, waiting for transfers between devices, from_root(): return lax.psum(block, axis)  914 us
    psum x2, waiting for transfers between devices, shards(): applied = lax.psum(product(matrix, column_vectors), 'col')  725 us
    psum x2, waiting for transfers between devices, shards(): inner = lax.psum(inner_tn(vectors, applied), 'row')  101 us
    psum x2, waiting for transfers between devices, shards(): gram = lax.psum(inner_tn(panel, panel), 'row')  76.5 us
    another operation x14, other arithmetic, coupling_of(): factor = jnp.linalg.cholesky(normal_eq)  69.4 us
    another operation x13, other arithmetic, solve_right(): lower = jnp.linalg.cholesky(gram)  68.7 us
    dot_general x8, matrix products, product(): jnp.dot(left, right, precision=lax.Precision.HIGHEST, preferred_element_t...  60.7 us
  transfers between devices with their start and end apart: 12, of which 12 were waited for; matrix products, arithmetic and copies ran while one was open for 1% of the time, Pallas kernels for 0%

commit v1 on v0

v1 whole, which is shorter than its diff:
```python
import jax
import jax.numpy as jnp
from jax import lax
from jax.experimental import pallas as pl
from jax.experimental.pallas import tpu as pltpu
from jax.sharding import Mesh, PartitionSpec as P

NB = 256
PIECE = 128
COL = ("z", "y", "xh")
ROW = ("xl", "c")
F32 = jnp.float32


def contract(left, right, dims, precision=lax.Precision.HIGHEST):
    return lax.dot_general(
        left, right, (dims, ((), ())), precision=precision, preferred_element_type=F32
    )


def nn(left, right):
    return contract(left, right, ((1,), (0,)))


def tn(left, right):
    return contract(left, right, ((0,), (0,)))


def nt(left, right):
    return contract(left, right, ((1,), (1,)))


def ring(block, axis, shift):
    return lax.ppermute(block, axis, [(k, (k + shift) % 4) for k in range(4)])


def swap(block, axis):
    return lax.ppermute(block, axis, [(0, 1), (1, 0)])


def row_sum(stacked):
    half = stacked.shape[0] // 2
    core = lax.axis_index("c")
    low, high = stacked[:half], stacked[half:]
    mine = jnp.where(core == 0, low, high) + swap(jnp.where(core == 0, high, low), "c")
    mine = mine + swap(mine, "xl")
    other = swap(mine, "c")
    return jnp.concatenate(
        [jnp.where(core == 0, mine, other), jnp.where(core == 0, other, mine)], 0
    )


def gather_rows(piece):
    z, y, xh = (lax.axis_index(a) for a in COL)
    other = swap(piece, "xh")
    pair = jnp.concatenate(
        [jnp.where(xh == 0, piece, other), jnp.where(xh == 0, other, piece)], 0
    )
    out = jnp.zeros((4, 4, 2 * PIECE, NB), F32)
    for half, (first, second) in enumerate((("y", "z"), ("z", "y"))):
        at_first, at_second = (y, z) if half == 0 else (z, y)
        own = pair[:, half * 128 : (half + 1) * 128]
        left, right = ring(own, first, 1), ring(own, first, 3)
        far = jnp.concatenate(
            [ring(left[:PIECE], first, 1), ring(right[PIECE:], first, 3)], 0
        )
        line = jnp.zeros((4, 2 * PIECE, 128), F32)
        for shift, block in ((0, own), (-1, left), (1, right), (2, far)):
            line = lax.dynamic_update_slice(line, block[None], ((at_first + shift) % 4, 0, 0))
        left, right = ring(line, second, 1), ring(line, second, 3)
        far = jnp.concatenate([ring(left[:2], second, 1), ring(right[2:], second, 3)], 0)
        for shift, block in ((0, line), (-1, left), (1, right), (2, far)):
            place = (at_second + shift) % 4
            if half == 0:
                out = lax.dynamic_update_slice(out, block[None], (place, 0, 0, 0))
            else:
                out = lax.dynamic_update_slice(out, block[:, None], (0, place, 0, 128))
    return out.reshape(32 * PIECE, NB)


def reduce_pieces(partial):
    xl, core = lax.axis_index("xl"), lax.axis_index("c")
    half = 2 * PIECE
    low, high = partial[:half], partial[half:]
    mine = jnp.where(core == 0, low, high) + swap(jnp.where(core == 0, high, low), "c")
    piece = 0.0
    for k in range(2):
        part = lax.dynamic_slice_in_dim(mine, ((xl + k) % 2) * PIECE, PIECE, 0)
        perm = [
            ((z * 2 + l) * 2 + c, (2 * c + (l + k) % 2) * 4 + z)
            for z in range(4)
            for l in range(2)
            for c in range(2)
        ]
        piece = piece + lax.ppermute(part, ("z", "xl", "c"), perm)
    mine = mine + swap(mine, "xl")
    other = swap(mine, "c")
    whole = jnp.concatenate(
        [jnp.where(core == 0, mine, other), jnp.where(core == 0, other, mine)], 0
    )
    return whole, piece


def scatter_pieces(block):
    piece = 0.0
    for q in range(4):
        perm = [(z * 4, q * 4 + z) for z in range(4)]
        piece = piece + lax.ppermute(
            block[q * PIECE : (q + 1) * PIECE], ("z", "xl", "c"), perm
        )
    return piece


def row_broadcast(block):
    first = lax.axis_index(ROW) == 0
    block = jnp.where(first, block, 0.0)
    block = block + swap(block, "xl")
    return block + swap(block, "c")


BF16 = jnp.bfloat16


def split(block):
    high = block.astype(BF16)
    return high, (block - high.astype(F32)).astype(BF16)


def split_outside(block):
    high = lax.reduce_precision(block, 8, 7)
    return high.astype(BF16), (block - high).astype(BF16)


def dot3(left, right):
    (lh, ll), (rh, rl) = left, right

    def dot(a, b):
        return jnp.dot(a, b, preferred_element_type=F32)

    return dot(lh, rh) + (dot(lh, rl) + dot(ll, rh))


def whole(shape):
    return pl.BlockSpec(shape, lambda b: (0,) * len(shape))


NATURAL = pl.BlockSpec((512, 512), lambda b: (b, 0))
GATHERED = pl.BlockSpec((4, 1, PIECE, NB), lambda b: (0, b, 0, 0))
GATHERED_SHAPE = jax.ShapeDtypeStruct((4, 8, PIECE, NB), F32)
SQUARE = jax.ShapeDtypeStruct((NB, NB), F32)
LARGE = pltpu.CompilerParams(vmem_limit_bytes=48 << 20)


def rows_of(ref):
    return ref[...].reshape(512, NB)


def blocks_of(array):
    return array.reshape(4, 8, PIECE, NB)


def product_kernel(m_ref, b_ref, out_ref, acc_ref):
    step = pl.program_id(0)

    @pl.when(step == 0)
    def _():
        acc_ref[...] = jnp.zeros_like(acc_ref)

    acc_ref[...] += dot3(split(rows_of(b_ref).T), split(m_ref[...]))

    @pl.when(step == pl.num_programs(0) - 1)
    def _():
        out_ref[...] = acc_ref[...].T


def product_of(matrix, base):
    return pl.pallas_call(
        product_kernel,
        grid=(8,),
        in_specs=[NATURAL, GATHERED],
        out_specs=whole((512, NB)),
        out_shape=jax.ShapeDtypeStruct((512, NB), F32),
        scratch_shapes=[pltpu.VMEM((NB, 512), F32)],
        compiler_params=LARGE,
        name="product",
    )(matrix, blocks_of(base))


def image_kernel(e_ref, w_ref, v_ref, h_ref, l_ref, out_ref, inner_ref):
    step = pl.program_id(0)

    @pl.when(step == 0)
    def _():
        inner_ref[...] = jnp.zeros_like(inner_ref)

    image = rows_of(e_ref) - dot3(split(rows_of(w_ref)), (h_ref[...], l_ref[...]))
    out_ref[...] = image.reshape(out_ref.shape)
    inner_ref[...] += dot3(split(image.T), split(rows_of(v_ref)))


def image_of(cols, product, vectors, inv):
    high, low = split_outside(inv.T)
    image, inner = pl.pallas_call(
        image_kernel,
        grid=(8,),
        in_specs=[GATHERED, GATHERED, GATHERED, whole((NB, NB)), whole((NB, NB))],
        out_specs=[GATHERED, whole((NB, NB))],
        out_shape=[GATHERED_SHAPE, SQUARE],
        compiler_params=LARGE,
        name="image",
    )(blocks_of(cols), blocks_of(product), blocks_of(vectors), high, low)
    return image.reshape(4096, NB), inner


def second_kernel(r_ref, e_ref, i_ref, v_ref, h_ref, l_ref, m_ref, base_ref, gram_ref, cross_ref, prod_ref, acc_ref):
    step = pl.program_id(0)

    @pl.when(step == 0)
    def _():
        gram_ref[...] = jnp.zeros_like(gram_ref)
        cross_ref[...] = jnp.zeros_like(cross_ref)
        acc_ref[...] = jnp.zeros_like(acc_ref)

    left = [split(rows_of(i_ref)), split(rows_of(v_ref))]
    base = rows_of(e_ref)
    for k in range(2):
        at = slice(k * NB, (k + 1) * NB)
        base = base - dot3(left[k], (h_ref[at, :], l_ref[at, :]))
    base = jnp.where((r_ref[0] == 0) & (step == 0), 0.0, base)
    base_ref[...] = base.reshape(base_ref.shape)
    turned = base.T
    parts = split(turned)
    gram_ref[...] += nn(turned, base)
    for k in range(2):
        cross_ref[:, k * NB : (k + 1) * NB] += dot3(parts, left[k])
    acc_ref[...] += dot3(parts, split(m_ref[...]))

    @pl.when(step == pl.num_programs(0) - 1)
    def _():
        prod_ref[...] = acc_ref[...].T


def second_of(row, cols, image, vectors, right, matrix):
    high, low = split_outside(right)
    base, gram, cross, product = pl.pallas_call(
        second_kernel,
        grid=(8,),
        in_specs=[
            pl.BlockSpec(memory_space=pltpu.SMEM),
            GATHERED,
            GATHERED,
            GATHERED,
            whole((2 * NB, NB)),
            whole((2 * NB, NB)),
            NATURAL,
        ],
        out_specs=[GATHERED, whole((NB, NB)), whole((NB, 2 * NB)), whole((512, NB))],
        out_shape=[
            GATHERED_SHAPE,
            SQUARE,
            jax.ShapeDtypeStruct((NB, 2 * NB), F32),
            jax.ShapeDtypeStruct((512, NB), F32),
        ],
        scratch_shapes=[pltpu.VMEM((NB, 512), F32)],
        compiler_params=LARGE,
        name="second",
    )(row[None], blocks_of(cols), blocks_of(image), blocks_of(vectors), high, low, matrix)
    return base.reshape(4096, NB), gram, cross, product


def update_kernel(m_ref, i_ref, v_ref, h_ref, l_ref, out_ref):
    out = m_ref[...]
    for k, ref in enumerate((i_ref, v_ref)):
        at = slice(k * NB, (k + 1) * NB)
        out = out - dot3(split(rows_of(ref)), (h_ref[at, :], l_ref[at, :]))
    out_ref[...] = out


def update_of(matrix, image, vectors, right):
    high, low = split_outside(right)
    return pl.pallas_call(
        update_kernel,
        grid=(8,),
        in_specs=[NATURAL, GATHERED, GATHERED, whole((512, 512)), whole((512, 512))],
        out_specs=NATURAL,
        out_shape=jax.ShapeDtypeStruct((4096, 512), F32),
        compiler_params=LARGE,
        name="update",
    )(matrix, blocks_of(image), blocks_of(vectors), high, low)


def diagonal_inverse(block, size):
    rows = lax.broadcasted_iota(jnp.int32, (size, 128), 0)
    lanes = lax.broadcasted_iota(jnp.int32, (size, 128), 1)
    work = jnp.where(lanes < size, block, (lanes - size == rows).astype(F32))
    for k in range(size - 1):
        pivot = work[k : k + 1, :]
        factor = work[:, k : k + 1] / pivot[:, k : k + 1]
        work = work - jnp.where(rows > k, factor, 0.0) * pivot
    diag = jnp.sum(jnp.where(lanes == rows, work, 0.0), axis=1, keepdims=True)
    return (work / jnp.sqrt(diag))[:, size : 2 * size]


def invert_factor(m_ref, x_ref, size=32):
    rows = lax.broadcasted_iota(jnp.int32, (NB, NB), 0)
    x_ref[...] = (rows == lax.broadcasted_iota(jnp.int32, (NB, NB), 1)).astype(F32)
    lane = lax.broadcasted_iota(jnp.int32, (size, NB), 1)
    for at in range(0, NB, size):
        strip = m_ref[at : at + size, :]
        block = strip[:, at // 128 * 128 : at // 128 * 128 + 128]
        if at % 128:
            block = pltpu.roll(block, 128 - at % 128, 1)
        inv = diagonal_inverse(block, size)
        strip = jnp.where(lane >= at, nn(inv, strip), 0.0)
        solved = nn(inv, x_ref[at : at + size, :])
        below = at + size
        if below < NB:
            left = strip.T[below:]
            m_ref[below:, :] -= nn(left, strip)
            x_ref[below:, :] -= nn(left, solved)
        x_ref[at : at + size, :] = solved


def factor_kernel(g_ref, inv_ref, m_ref):
    m_ref[...] = g_ref[...]
    invert_factor(m_ref, inv_ref)


def inverse_factor(gram):
    return pl.pallas_call(
        factor_kernel,
        out_shape=SQUARE,
        scratch_shapes=[pltpu.VMEM((NB, NB), F32)],
        name="factor",
    )(gram)


def coupling_kernel(t_ref, inv_ref, top_ref, out_ref, m_ref, f_ref):
    rows = lax.broadcasted_iota(jnp.int32, (NB, NB), 0)
    eye = (rows == lax.broadcasted_iota(jnp.int32, (NB, NB), 1)).astype(F32)
    top = eye - nt(t_ref[...], inv_ref[...])
    top_ref[...] = top
    m_ref[...] = nt(top, top)
    invert_factor(m_ref, f_ref)
    factor = f_ref[...]
    out_ref[...] = nn(factor.T, nn(factor, top))


def coupling_of(base_top, inv):
    return pl.pallas_call(
        coupling_kernel,
        out_shape=(SQUARE, SQUARE),
        scratch_shapes=[pltpu.VMEM((NB, NB), F32)] * 2,
        name="coupling",
    )(base_top, inv)


def shards(matrix):
    z, y, xh = (lax.axis_index(a) for a in COL)
    row = lax.axis_index(ROW)
    on_first = row == 0
    lanes = jnp.arange(NB, dtype=jnp.int32)[None, :]

    where_in = jnp.arange(32 * PIECE, dtype=jnp.int32)
    gathered_rows = (
        row * 4096
        + (where_in // 256 % 4 * 2 + where_in // 128 % 2) * 512
        + where_in // 1024 * 128
        + where_in % 128
    )[:, None]
    column_rows = (((z * 4 + y) * 2 + xh) * 512 + jnp.arange(512, dtype=jnp.int32))[:, None]
    piece_rows = (
        row * 4096 + (y * 2 + xh) * 512 + z * 128 + jnp.arange(128, dtype=jnp.int32)
    )[:, None]

    def unit(rows, first):
        return (rows - first == lanes).astype(F32)

    def rows_at(block, first):
        cube = block.reshape(4, 8, PIECE, NB)
        at = first // 512
        q = first % 512 // 128
        return jnp.where(on_first, jnp.concatenate([cube[q, at], cube[q + 1, at]], 0), 0.0)

    def high(dims, left, right):
        return contract(left, right, dims, lax.Precision.HIGH)

    wide_nt = ((1,), (1,))

    strip = matrix[: 3 * NB].T
    pieces = scatter_pieces(strip[:, : 2 * NB])
    base_piece = jnp.where(piece_rows >= NB, pieces[:, :NB], 0.0)
    next_piece = pieces[:, NB:]
    next_cols = lax.all_gather(next_piece, COL, tiled=True)
    base = gather_rows(base_piece)
    strip, base = lax.optimization_barrier((strip, base))

    product_j, product_p = reduce_pieces(product_of(matrix, base))
    stat = row_sum(
        jnp.concatenate([tn(base, base), rows_at(base, 256), rows_at(base, 512)], 0)
    )
    product = gather_rows(product_p)
    last_piece = scatter_pieces(strip[:, 2 * NB :])
    strip = row_broadcast(strip)
    inv = inverse_factor(stat[:256])
    top, coupling = coupling_of(stat[256:512], inv)
    top_next = -nt(stat[512:768], inv)
    vectors = unit(gathered_rows, 256) - high(wide_nt, base, inv)

    image, inner = image_of(next_cols, product, vectors, inv)
    stat = row_sum(jnp.concatenate([inner, rows_at(image, 256), rows_at(image, 512)], 0))
    inner = nn(tn(coupling, stat[:256]), coupling)
    image_top, image_next = stat[256:512], stat[512:]

    def factors(vec, img):
        return nt(coupling, vec), tn(coupling, img.T) - nt(inner, vec)

    right = jnp.concatenate(factors(top, image_top), 0)
    base2, gram, cross, partial = second_of(row, next_cols, image, vectors, right, matrix)
    stat = row_sum(jnp.concatenate([gram, rows_at(base2, 512)], 0))
    product_j2, product_p2 = reduce_pieces(partial)
    cross = row_sum(cross.T)
    inv2 = inverse_factor(stat[:256])
    mix_v = tn(coupling, cross[:256]) - nn(inner, cross[256:])
    mix_i = nn(coupling, cross[256:])
    next_a, next_b = factors(top_next, image_next)

    def second_image(cols, base_rows, first, prod1, prod2, rows):
        vec = unit(rows, 256) - nt(base_rows, inv)
        img = first - nt(prod1, inv)
        prod = prod2 - nn(vec, mix_v) - nn(img, mix_i)
        return vec, img, cols - nn(img, next_a) - nn(vec, next_b) - nt(prod, inv2)

    image2_p = second_image(last_piece, base_piece, next_piece, product_p, product_p2, piece_rows)[2]
    image2 = gather_rows(image2_p)

    base_j = jnp.where(column_rows >= 256, strip[:, :256], 0.0)
    vectors_j, image_j, image2_j = second_image(
        strip[:, 512:], base_j, strip[:, 256:512], product_j, product_j2, column_rows
    )
    top2, coupling2 = coupling_of(stat[256:], inv2)
    base2_j = jnp.where(
        column_rows >= 512,
        strip[:, 256:512] - nn(image_j, right[:256]) - nn(vectors_j, right[256:]),
        0.0,
    )
    vectors2 = unit(gathered_rows, 512) - high(wide_nt, base2, inv2)
    vectors2_j = unit(column_rows, 512) - nt(base2_j, inv2)
    first = update_of(
        matrix, image, vectors, jnp.concatenate(factors(vectors_j, image_j), 0)
    )

    inner2 = row_sum(high(((0,), (0,)), vectors2, image2))
    inner2 = nn(tn(coupling2, inner2), coupling2)
    last = jnp.concatenate(
        [nt(coupling2, vectors2_j), tn(coupling2, image2_j.T) - nt(inner2, vectors2_j)], 0
    )
    return update_of(first, image2, vectors2, last)


def solution(mesh):
    fine = Mesh(mesh.devices.reshape(4, 4, 2, 2, 2), COL + ROW)
    return jax.shard_map(
        shards,
        mesh=fine,
        in_specs=(P(ROW, COL),),
        out_specs=P(ROW, COL),
        check_vma=False,
    )
```

time: 2290 us -> 574 us (0.25)
  waiting for transfers between devices: 1820 us -> 118 us
  other arithmetic: 239 us -> 19.3 us
  Pallas kernels: 0 us -> 180 us
  starting transfers between devices: 1.67 us -> 152 us
  matrix products: 145 us -> 54.6 us
  local copies, waits for them, and re-layouts: 65.9 us -> 26.5 us
    psum x12 -> x0, waiting for transfers between devices: 1820 us -> none  [the longest x6 914 us: from_root(): return lax.psum(block, axis)]
    another operation x36 -> x0, other arithmetic: 217 us -> none  [the longest x14 69.4 us: coupling_of(): factor = jnp.linalg.cholesky(normal_eq)]
    pallas_call x0 -> x9, Pallas kernels: none -> 180 us  [the longest x2 59.5 us: coupling_of(): pl.pallas_call(coupling_kernel, out_shape=(SQUARE, SQUARE), scratch_shape...]
    ppermute x0 -> x86, starting transfers between devices: none -> 152 us  [the longest x48 74.5 us: ring(): return lax.ppermute(block, axis, [(k, (k + shift) % 4) for k in range(4)])]
    ppermute x0 -> x86, waiting for transfers between devices: none -> 118 us  [the longest x26 75.6 us: swap(): return lax.ppermute(block, axis, [(0, 1), (1, 0)])]
    dot_general x18 -> x41, matrix products: 124 us -> 54.6 us  [contract(): lax.dot_general(left, right, (dims, ((), ())), precision=precision, prefe...]
  transfers between devices with their start and end apart: 12 -> 87, of which waited for: 12 -> 23; matrix products, arithmetic and copies ran while one was open for 1% -> 15% of each run, Pallas kernels for 0% -> 30%
where the time goes in v1:
time: 574 us; the launch traced here: 565 us
  Pallas kernels  180 us (31%)
  starting transfers between devices  152 us (26%)
  waiting for transfers between devices  118 us (21%)
  matrix products  54.6 us (10%)
  local copies, waits for them, and re-layouts  26.5 us (5%)
  other arithmetic  19.3 us (3%)
  between operations  15.6 us (3%)
    ppermute x26, waiting for transfers between devices, swap(): return lax.ppermute(block, axis, [(0, 1), (1, 0)])  75.6 us
    ppermute x48, starting transfers between devices, ring(): return lax.ppermute(block, axis, [(k, (k + shift) % 4) for k in range(4)])  74.5 us
    pallas_call x2, Pallas kernels, coupling_of(): pl.pallas_call(coupling_kernel, out_shape=(SQUARE, SQUARE), scratch_shape...  59.5 us
    pallas_call x2, Pallas kernels, inverse_factor(): pl.pallas_call(factor_kernel, out_shape=SQUARE, scratch_shapes=[pltpu.VME...  55.3 us
    ppermute x26, starting transfers between devices, swap(): return lax.ppermute(block, axis, [(0, 1), (1, 0)])  55 us
    dot_general x41, matrix products, contract(): lax.dot_general(left, right, (dims, ((), ())), precision=precision, prefe...  54.6 us
    ppermute x48, waiting for transfers between devices, ring(): return lax.ppermute(block, axis, [(k, (k + shift) % 4) for k in range(4)])  28.1 us
    pallas_call x2, Pallas kernels, update_of(): pl.pallas_call(update_kernel, grid=(8,), in_specs=[NATURAL, GATHERED, GAT...  25.9 us
  transfers between devices with their start and end apart: 87, of which 23 were waited for; matrix products, arithmetic and copies ran while one was open for 15% of the time, Pallas kernels for 30%

profile of v1, /device:TPU:1, one launch (start us, length us, event | category | flops | bytes accessed | tf_op | source)
XLA Modules:
  0.0 565.1 jit_solution(17004232842695672302)
XLA Ops:
  14.2 5.0 collective-permute-done
  19.9 2.9 collective-permute-start.4
  25.5 9.0 %collective-permute-start.14 = (f32[256,128]{1,0:T(8,128)S(1)}, f32[256,128]{1,0:T(8,128)S(1)}, u32[]{:S(2)}, u32[]{:S(2)}) collective-permute-start(f32[256,128]{1,0:T(8,128)S(1)} %get-tuple-element.36), channel_id=1, source_target_pairs={{0,96},{32,0},{64,32},{96,64},{1,97},{33,1},{65,33},{97,65},{2,98}... | collective-permute-start | bytes 393224 | tf_op jit(solution)/shard_map/ppermute | solution.py:34
  62.3 3.6 collective-permute-done.11
  69.0 9.8 %product.1 = f32[512,256]{1,0:T(8,128)S(1)} custom-call(f32[4096,512]{1,0:T(8,128)} %m_ref.5, f32[4,8,128,256]{3,2,1,0:T(8,128)S(1)} %bitcast.246), custom_call_target="tpu_custom_call" | custom-call | tf_op jit(solution)/shard_map/product/pallas_call | solution.py:177
  78.8 11.5 %collective-permute-start.21 = (f32[256,256]{1,0:T(8,128)S(1)}, f32[256,256]{1,0:T(8,128)S(1)}, u32[]{:S(2)}, u32[]{:S(2)}) collective-permute-start(f32[256,256]{1,0:T(8,128)S(1)} %slice_select_fusion.3), channel_id=1, source_target_pairs={{0,1},{1,0},{2,3},{3,2},{4,5},{5,4},{6,7},{7,6},{8,9},{9,8},{10,11... | collective-permute-start | bytes 786440 | tf_op jit(solution)/shard_map/ppermute | solution.py:38
  90.4 6.8 %fusion.90 = f32[256,256]{1,0:T(8,128)S(1)} fusion(f32[4096,256]{1,0:T(8,128)S(1)} %bitcast.247), kind=kOutput, calls=%fused_computation.254 | convolution fusion | flops 3221225472 | bytes 4456448 | tf_op jit(solution)/shard_map/dot_general | solution.py:16
  99.6 4.5 collective-permute-start.23
  105.4 4.9 collective-permute-done.22
  116.8 3.5 collective-permute-start.42
  120.4 52.3 %collective-permute-done.46 = f32[256,256]{1,0:T(8,128)S(1)} collective-permute-done((f32[256,256]{1,0:T(8,128)S(1)}, f32[256,256]{1,0:T(8,128)S(1)}, u32[]{:S(2)}, u32[]{:S(2)}) %collective-permute-start.46) | collective-permute-done | bytes 262176 | tf_op jit(solution)/shard_map/ppermute | solution.py:38
  176.6 3.6 collective-permute-done.33
  193.0 3.2 collective-permute-start.43
  206.7 27.6 %factor.2.inv_ref = f32[256,256]{1,0:T(8,128)} custom-call(f32[256,256]{1,0:T(8,128)} %get-tuple-element.74.g_ref), custom_call_target="tpu_custom_call" | custom-call | tf_op jit(solution)/shard_map/factor/pallas_call | solution.py:330
  237.7 5.8 %convolution_subtract_fusion.1 = f32[4096,256]{1,0:T(8,128)} fusion(f32[4096,256]{1,0:T(8,128)} %bitcast.249, f32[256,256]{1,0:T(8,128)} %factor.2.inv_ref, s32[4096]{0:T(1024)S(1)} %copy-done.39), kind=kOutput, calls=%fused_computation.1 | convolution fusion | flops 1613758464 | bytes 8667136 | tf_op jit(solution)/shard_map/dot_general | solution.py:16
  246.4 29.7 %coupling.2 = (f32[256,256]{1,0:T(8,128)}, f32[256,256]{1,0:T(8,128)}) custom-call(f32[256,256]{1,0:T(8,128)} %get-tuple-element.73.t_ref, f32[256,256]{1,0:T(8,128)} %factor.2.inv_ref), custom_call_target="tpu_custom_call" | custom-call | tf_op jit(solution)/shard_map/coupling/pallas_call | solution.py:350
  297.2 5.3 collective-permute-start.45
  307.1 11.1 %image.1 = (f32[4,8,128,256]{3,2,1,0:T(8,128)S(1)}, f32[256,256]{1,0:T(8,128)S(1)}) custom-call(f32[4,8,128,256]{3,2,1,0:T(8,128)} %bitcast.261, f32[4,8,128,256]{3,2,1,0:T(8,128)} %bitcast.44.w_ref, f32[4,8,128,256]{3,2,1,0:T(8,128)} %bitcast.253, bf16[256,256]{1,0:T(8,128)(2,1)S(1)} %get-tuple-element.82.h_ref, bf16[256,256]{1,0:T(8,128)(2,1)S(1)} %get-tuple-element.81.l_ref), custom_call_target="tpu_custom_call" | custom-call | tf_op jit(solution)/shard_map/image/pallas_call | solution.py:203
  323.3 8.7 %collective-permute-done.49 = f32[384,256]{1,0:T(8,128)S(1)} collective-permute-done((f32[384,256]{1,0:T(8,128)S(1)}, f32[384,256]{1,0:T(8,128)S(1)}, u32[]{:S(2)}, u32[]{:S(2)}) %collective-permute-start.49) | collective-permute-done | bytes 393248 | tf_op jit(solution)/shard_map/ppermute | solution.py:38
  341.9 18.1 %second.1 = (f32[4,8,128,256]{3,2,1,0:T(8,128)S(1)}, f32[256,256]{1,0:T(8,128)S(1)}, f32[256,512]{1,0:T(8,128)S(1)}, f32[512,256]{1,0:T(8,128)S(1)}) custom-call(s32[1]{0:T(128)} %bitcast.55.r_ref, f32[4,8,128,256]{3,2,1,0:T(8,128)} %bitcast.262, f32[4,8,128,256]{3,2,1,0:T(8,128)} %copy-done.3, f32[4,8,128,256]{3,2,1,0:T(8,128)} %bitcast.254, ...), custom_call_target="tpu_custom_call" | custom-call | tf_op jit(solution)/shard_map/second/pallas_call | solution.py:245
  371.8 13.0 %update.2.m_ref = f32[4096,512]{1,0:T(8,128)} custom-call(f32[4096,512]{1,0:T(8,128)} %m_ref.5, f32[4,8,128,256]{3,2,1,0:T(8,128)S(1)} %copy-done.4, f32[4,8,128,256]{3,2,1,0:T(8,128)} %bitcast.255, bf16[512,512]{1,0:T(8,128)(2,1)S(1)} %get-tuple-element.60.h_ref, bf16[512,512]{1,0:T(8,128)(2,1)S(1)} %get-tuple-element.59.l_ref), custom_call_target="tpu_custom_call" | custom-call | tf_op jit(solution)/shard_map/update/pallas_call | solution.py:281
  388.7 4.4 collective-permute-done.62
  407.8 27.6 %factor.3.inv_ref = f32[256,256]{1,0:T(8,128)} custom-call(f32[256,256]{1,0:T(8,128)} %get-tuple-element.68.g_ref), custom_call_target="tpu_custom_call" | custom-call | tf_op jit(solution)/shard_map/factor/pallas_call | solution.py:330
  435.4 7.0 %collective-permute-start.56 = (f32[128,256]{1,0:T(8,128)}, f32[128,256]{1,0:T(8,128)S(1)}, u32[]{:S(2)}, u32[]{:S(2)}) collective-permute-start(f32[128,256]{1,0:T(8,128)} %get-tuple-element.80), channel_id=1, source_target_pairs={{0,0},{1,64},{2,32},{3,96},{32,1},{33,65},{34,33},{35,97},{64,2},{... | collective-permute-start | bytes 393224 | tf_op jit(solution)/shard_map/ppermute | solution.py:95
  445.7 4.0 collective-permute-done.57
  477.9 4.2 collective-permute-done.69
  485.1 2.9 collective-permute-start.80
  492.2 3.4 fusion.108
  495.7 6.4 %collective-permute-start.83 = (f32[128,256]{1,0:T(8,128)S(1)}, f32[128,256]{1,0:T(8,128)S(1)}, u32[]{:S(2)}, u32[]{:S(2)}) collective-permute-start(f32[128,256]{1,0:T(8,128)S(1)} %slice_select_fusion.6), channel_id=1, source_target_pairs={{0,1},{1,0},{2,3},{3,2},{4,5},{5,4},{6,7},{7,6},{8,9},{9,8},{10,11... | collective-permute-start | bytes 393224 | tf_op jit(solution)/shard_map/ppermute | solution.py:38
  502.7 29.8 %coupling.3 = (f32[256,256]{1,0:T(8,128)}, f32[256,256]{1,0:T(8,128)}) custom-call(f32[256,256]{1,0:T(8,128)} %get-tuple-element.67.t_ref, f32[256,256]{1,0:T(8,128)} %factor.3.inv_ref), custom_call_target="tpu_custom_call" | custom-call | tf_op jit(solution)/shard_map/coupling/pallas_call | solution.py:350
  535.4 3.2 collective-permute-done.84
  545.1 12.9 %update.3 = f32[4096,512]{1,0:T(8,128)} custom-call(f32[4096,512]{1,0:T(8,128)} %update.2.m_ref, f32[4,8,128,256]{3,2,1,0:T(8,128)S(1)} %bitcast.251, f32[4,8,128,256]{3,2,1,0:T(8,128)} %bitcast.256, bf16[512,512]{1,0:T(8,128)(2,1)S(1)} %get-tuple-element.58.h_ref, bf16[512,512]{1,0:T(8,128)(2,1)S(1)} %get-tuple-element.57.l_ref), custom_call_target="tpu_custom_call" | custom-call | tf_op jit(solution)/shard_map/update/pallas_call | solution.py:281
  (426 shorter events, 203.6 us)
Async XLA Ops:
  6.5 300.6 %all-gather.2.cloned.1.call-start = ((), (), s32[]{:S(2)}) async-start(), calls=%async_computation | async-start | bytes 4325376 | tf_op jit(solution)/shard_map/all_gather | solution.py:394
  25.4 13.2 %collective-permute-start.13 = (f32[256,128]{1,0:T(8,128)S(1)}, f32[256,128]{1,0:T(8,128)S(1)}, u32[]{:S(2)}, u32[]{:S(2)}) collective-permute-start(f32[256,128]{1,0:T(8,128)S(1)} %get-tuple-element.36), channel_id=1, source_target_pairs={{0,32},{32,64},{64,96},{96,0},{1,33},{33,65},{65,97},{97,1},{2,34}... | collective-permute-start | bytes 393224 | tf_op jit(solution)/shard_map/ppermute | solution.py:34
  25.5 13.2 %collective-permute-start.14 = (f32[256,128]{1,0:T(8,128)S(1)}, f32[256,128]{1,0:T(8,128)S(1)}, u32[]{:S(2)}, u32[]{:S(2)}) collective-permute-start(f32[256,128]{1,0:T(8,128)S(1)} %get-tuple-element.36), channel_id=1, source_target_pairs={{0,96},{32,0},{64,32},{96,64},{1,97},{33,1},{65,33},{97,65},{2,98}... | collective-permute-start | bytes 393224 | tf_op jit(solution)/shard_map/ppermute | solution.py:34
  78.8 18.6 %collective-permute-start.21 = (f32[256,256]{1,0:T(8,128)S(1)}, f32[256,256]{1,0:T(8,128)S(1)}, u32[]{:S(2)}, u32[]{:S(2)}) collective-permute-start(f32[256,256]{1,0:T(8,128)S(1)} %slice_select_fusion.3), channel_id=1, source_target_pairs={{0,1},{1,0},{2,3},{3,2},{4,5},{5,4},{6,7},{7,6},{8,9},{9,8},{10,11... | collective-permute-start | bytes 786440 | tf_op jit(solution)/shard_map/ppermute | solution.py:38
  97.3 19.4 %collective-permute-start.41 = (f32[384,256]{1,0:T(8,128)S(1)}, f32[384,256]{1,0:T(8,128)S(1)}, u32[]{:S(2)}, u32[]{:S(2)}) collective-permute-start(f32[384,256]{1,0:T(8,128)S(1)} %fusion.35), channel_id=1, source_target_pairs={{0,1},{1,0},{2,3},{3,2},{4,5},{5,4},{6,7},{7,6},{8,9},{9,8},{10,11... | collective-permute-start | bytes 1179656 | tf_op jit(solution)/shard_map/ppermute | solution.py:38
  97.5 12.7 %collective-permute-start.22 = (f32[128,256]{1,0:T(8,128)S(1)}, f32[128,256]{1,0:T(8,128)S(1)}, u32[]{:S(2)}, u32[]{:S(2)}) collective-permute-start(f32[128,256]{1,0:T(8,128)S(1)} %get-tuple-element.86), channel_id=1, source_target_pairs={{0,0},{1,64},{2,32},{3,96},{32,1},{33,65},{34,33},{35,97},{64,2},{... | collective-permute-start | bytes 393224 | tf_op jit(solution)/shard_map/ppermute | solution.py:95
  112.5 183.1 %collective-permute-start.44 = (f32[512,768]{1,0:T(8,128)}, f32[512,768]{1,0:T(8,128)}, u32[]{:S(2)}, u32[]{:S(2)}) collective-permute-start(f32[512,768]{1,0:T(8,128)} %broadcast_select_fusion), channel_id=1, source_target_pairs={{0,2},{2,0},{1,3},{3,1},{4,6},{6,4},{5,7},{7,5},{8,10},{10,8},{9,1... | collective-permute-start | bytes 4718600 | tf_op jit(solution)/shard_map/ppermute | solution.py:38
  115.3 57.4 %collective-permute-start.46 = (f32[256,256]{1,0:T(8,128)S(1)}, f32[256,256]{1,0:T(8,128)S(1)}, u32[]{:S(2)}, u32[]{:S(2)}) collective-permute-start(f32[256,256]{1,0:T(8,128)S(1)} %select_add_fusion.5), channel_id=1, source_target_pairs={{0,2},{2,0},{1,3},{3,1},{4,6},{6,4},{5,7},{7,5},{8,10},{10,8},{9,1... | collective-permute-start | bytes 786440 | tf_op jit(solution)/shard_map/ppermute | solution.py:38
  115.9 58.1 %collective-permute-start.25 = (f32[256,128]{1,0:T(8,128)S(1)}, f32[256,128]{1,0:T(8,128)S(1)}, u32[]{:S(2)}, u32[]{:S(2)}) collective-permute-start(f32[256,128]{1,0:T(8,128)S(1)} %get-tuple-element.34), channel_id=1, source_target_pairs={{0,8},{8,16},{16,24},{24,0},{1,9},{9,17},{17,25},{25,1},{2,10},{10... | collective-permute-start | bytes 393224 | tf_op jit(solution)/shard_map/ppermute | solution.py:34
  116.8 76.1 %collective-permute-start.42 = (f32[384,256]{1,0:T(8,128)S(1)}, f32[384,256]{1,0:T(8,128)S(1)}, u32[]{:S(2)}, u32[]{:S(2)}) collective-permute-start(f32[384,256]{1,0:T(8,128)S(1)} %select_add_fusion.1), channel_id=1, source_target_pairs={{0,2},{2,0},{1,3},{3,1},{4,6},{6,4},{5,7},{7,5},{8,10},{10,8},{9,1... | collective-permute-start | bytes 1179656 | tf_op jit(solution)/shard_map/ppermute | solution.py:38
  172.7 29.4 %collective-permute-start.47 = (f32[256,256]{1,0:T(8,128)S(1)}, f32[256,256]{1,0:T(8,128)S(1)}, u32[]{:S(2)}, u32[]{:S(2)}) collective-permute-start(f32[256,256]{1,0:T(8,128)S(1)} %add.506), channel_id=1, source_target_pairs={{0,1},{1,0},{2,3},{3,2},{4,5},{5,4},{6,7},{7,6},{8,9},{9,8},{10,11... | collective-permute-start | bytes 786440 | tf_op jit(solution)/shard_map/ppermute | solution.py:38
  199.5 78.8 %collective-permute-start.29 = (f32[4,256,128]{2,1,0:T(8,128)S(1)}, f32[4,256,128]{2,1,0:T(8,128)}, u32[]{:S(2)}, u32[]{:S(2)}) collective-permute-start(f32[4,256,128]{2,1,0:T(8,128)S(1)} %fusion.43), channel_id=1, source_target_pairs={{0,32},{32,64},{64,96},{96,0},{1,33},{33,65},{65,97},{97,1},{2,34}... | collective-permute-start | bytes 1572872 | tf_op jit(solution)/shard_map/ppermute | solution.py:34
  199.5 79.8 %collective-permute-start.30 = (f32[4,256,128]{2,1,0:T(8,128)S(1)}, f32[4,256,128]{2,1,0:T(8,128)}, u32[]{:S(2)}, u32[]{:S(2)}) collective-permute-start(f32[4,256,128]{2,1,0:T(8,128)S(1)} %fusion.43), channel_id=1, source_target_pairs={{0,96},{32,0},{64,32},{96,64},{1,97},{33,1},{65,33},{97,65},{2,98}... | collective-permute-start | bytes 1572872 | tf_op jit(solution)/shard_map/ppermute | solution.py:34
  202.2 82.7 %collective-permute-start.37 = (f32[4,256,128]{2,1,0:T(8,128)S(1)}, f32[4,256,128]{2,1,0:T(8,128)}, u32[]{:S(2)}, u32[]{:S(2)}) collective-permute-start(f32[4,256,128]{2,1,0:T(8,128)S(1)} %fusion.44), channel_id=1, source_target_pairs={{0,8},{8,16},{16,24},{24,0},{1,9},{9,17},{17,25},{25,1},{2,10},{10... | collective-permute-start | bytes 1572872 | tf_op jit(solution)/shard_map/ppermute | solution.py:34
  203.1 84.0 %collective-permute-start.38 = (f32[4,256,128]{2,1,0:T(8,128)S(1)}, f32[4,256,128]{2,1,0:T(8,128)}, u32[]{:S(2)}, u32[]{:S(2)}) collective-permute-start(f32[4,256,128]{2,1,0:T(8,128)S(1)} %fusion.44), channel_id=1, source_target_pairs={{0,24},{8,0},{16,8},{24,16},{1,25},{9,1},{17,9},{25,17},{2,26},{10... | collective-permute-start | bytes 1572872 | tf_op jit(solution)/shard_map/ppermute | solution.py:34
  279.2 12.1 %collective-permute-start.31 = (f32[2,256,128]{2,1,0:T(8,128)S(1)}, f32[2,256,128]{2,1,0:T(8,128)S(1)}, u32[]{:S(2)}, u32[]{:S(2)}) collective-permute-start(f32[2,256,128]{2,1,0:T(8,128)S(1)} %slice.325), channel_id=1, source_target_pairs={{0,32},{32,64},{64,96},{96,0},{1,33},{33,65},{65,97},{97,1},{2,34}... | collective-permute-start | bytes 786440 | tf_op jit(solution)/shard_map/ppermute | solution.py:34
  284.9 159.3 %collective-permute-start.51 = (f32[128,256]{1,0:T(8,128)}, f32[128,256]{1,0:T(8,128)}, u32[]{:S(2)}, u32[]{:S(2)}) collective-permute-start(f32[128,256]{1,0:T(8,128)} %get-tuple-element.52), channel_id=1, source_target_pairs={{0,0},{32,1},{64,2},{96,3},{4,4},{36,5},{68,6},{100,7},{8,8},{40,9... | collective-permute-start | bytes 393224 | tf_op jit(solution)/shard_map/ppermute | solution.py:108
  287.1 157.4 %collective-permute-start.52 = (f32[128,256]{1,0:T(8,128)}, f32[128,256]{1,0:T(8,128)}, u32[]{:S(2)}, u32[]{:S(2)}) collective-permute-start(f32[128,256]{1,0:T(8,128)} %get-tuple-element.49), channel_id=1, source_target_pairs={{0,32},{32,33},{64,34},{96,35},{4,36},{36,37},{68,38},{100,39},{8,... | collective-permute-start | bytes 393224 | tf_op jit(solution)/shard_map/ppermute | solution.py:108
  291.3 15.0 %collective-permute-start.39 = (f32[2,256,128]{2,1,0:T(8,128)S(1)}, f32[2,256,128]{2,1,0:T(8,128)S(1)}, u32[]{:S(2)}, u32[]{:S(2)}) collective-permute-start(f32[2,256,128]{2,1,0:T(8,128)S(1)} %slice.329), channel_id=1, source_target_pairs={{0,8},{8,16},{16,24},{24,0},{1,9},{9,17},{17,25},{25,1},{2,10},{10... | collective-permute-start | bytes 786440 | tf_op jit(solution)/shard_map/ppermute | solution.py:34
  291.3 15.0 %collective-permute-start.40 = (f32[2,256,128]{2,1,0:T(8,128)S(1)}, f32[2,256,128]{2,1,0:T(8,128)S(1)}, u32[]{:S(2)}, u32[]{:S(2)}) collective-permute-start(f32[2,256,128]{2,1,0:T(8,128)S(1)} %slice.330), channel_id=1, source_target_pairs={{0,24},{8,0},{16,8},{24,16},{1,25},{9,1},{17,9},{25,17},{2,26},{10... | collective-permute-start | bytes 786440 | tf_op jit(solution)/shard_map/ppermute | solution.py:34
  297.2 22.9 %collective-permute-start.45 = (f32[512,768]{1,0:T(8,128)S(1)}, f32[512,768]{1,0:T(8,128)}, u32[]{:S(2)}, u32[]{:S(2)}) collective-permute-start(f32[512,768]{1,0:T(8,128)S(1)} %fusion.180), channel_id=1, source_target_pairs={{0,1},{1,0},{2,3},{3,2},{4,5},{5,4},{6,7},{7,6},{8,9},{9,8},{10,11... | collective-permute-start | bytes 4718600 | tf_op jit(solution)/shard_map/ppermute | solution.py:38
  362.8 22.0 %collective-permute-start.61 = (f32[256,256]{1,0:T(8,128)}, f32[256,256]{1,0:T(8,128)}, u32[]{:S(2)}, u32[]{:S(2)}) collective-permute-start(f32[256,256]{1,0:T(8,128)} %fusion.37), channel_id=1, source_target_pairs={{0,1},{1,0},{2,3},{3,2},{4,5},{5,4},{6,7},{7,6},{8,9},{9,8},{10,11... | collective-permute-start | bytes 786440 | tf_op jit(solution)/shard_map/ppermute | solution.py:38
  365.6 22.0 %collective-permute-start.55 = (f32[256,256]{1,0:T(8,128)}, f32[256,256]{1,0:T(8,128)}, u32[]{:S(2)}, u32[]{:S(2)}) collective-permute-start(f32[256,256]{1,0:T(8,128)} %slice_select_fusion.4), channel_id=1, source_target_pairs={{0,1},{1,0},{2,3},{3,2},{4,5},{5,4},{6,7},{7,6},{8,9},{9,8},{10,11... | collective-permute-start | bytes 786440 | tf_op jit(solution)/shard_map/ppermute | solution.py:38
  366.3 19.6 %collective-permute-start.58 = (f32[256,256]{1,0:T(8,128)S(1)}, f32[256,256]{1,0:T(8,128)S(1)}, u32[]{:S(2)}, u32[]{:S(2)}) collective-permute-start(f32[256,256]{1,0:T(8,128)S(1)} %slice_select_fusion.2), channel_id=1, source_target_pairs={{0,1},{1,0},{2,3},{3,2},{4,5},{5,4},{6,7},{7,6},{8,9},{9,8},{10,11... | collective-permute-start | bytes 786440 | tf_op jit(solution)/shard_map/ppermute | solution.py:38
  386.0 12.7 %collective-permute-start.59 = (f32[256,256]{1,0:T(8,128)S(1)}, f32[256,256]{1,0:T(8,128)S(1)}, u32[]{:S(2)}, u32[]{:S(2)}) collective-permute-start(f32[256,256]{1,0:T(8,128)S(1)} %select_add_fusion.3), channel_id=1, source_target_pairs={{0,2},{2,0},{1,3},{3,1},{4,6},{6,4},{5,7},{7,5},{8,10},{10,8},{9,1... | collective-permute-start | bytes 786440 | tf_op jit(solution)/shard_map/ppermute | solution.py:38
  388.5 15.7 %collective-permute-start.81 = (f32[256,256]{1,0:T(8,128)S(1)}, f32[256,256]{1,0:T(8,128)S(1)}, u32[]{:S(2)}, u32[]{:S(2)}) collective-permute-start(f32[256,256]{1,0:T(8,128)S(1)} %select_add_fusion.4), channel_id=1, source_target_pairs={{0,2},{2,0},{1,3},{3,1},{4,6},{6,4},{5,7},{7,5},{8,10},{10,8},{9,1... | collective-permute-start | bytes 786440 | tf_op jit(solution)/shard_map/ppermute | solution.py:38
  393.1 12.5 %collective-permute-start.63 = (f32[256,256]{1,0:T(8,128)S(1)}, f32[256,256]{1,0:T(8,128)S(1)}, u32[]{:S(2)}, u32[]{:S(2)}) collective-permute-start(f32[256,256]{1,0:T(8,128)S(1)} %add.517), channel_id=1, source_target_pairs={{0,1},{1,0},{2,3},{3,2},{4,5},{5,4},{6,7},{7,6},{8,9},{9,8},{10,11... | collective-permute-start | bytes 786440 | tf_op jit(solution)/shard_map/ppermute | solution.py:38
  398.7 36.7 %collective-permute-start.60 = (f32[256,256]{1,0:T(8,128)S(1)}, f32[256,256]{1,0:T(8,128)S(1)}, u32[]{:S(2)}, u32[]{:S(2)}) collective-permute-start(f32[256,256]{1,0:T(8,128)S(1)} %add.515), channel_id=1, source_target_pairs={{0,1},{1,0},{2,3},{3,2},{4,5},{5,4},{6,7},{7,6},{8,9},{9,8},{10,11... | collective-permute-start | bytes 786440 | tf_op jit(solution)/shard_map/ppermute | solution.py:38
  404.3 41.4 %collective-permute-start.53 = (f32[128,256]{1,0:T(8,128)}, f32[128,256]{1,0:T(8,128)}, u32[]{:S(2)}, u32[]{:S(2)}) collective-permute-start(f32[128,256]{1,0:T(8,128)} %get-tuple-element.51), channel_id=1, source_target_pairs={{0,64},{32,65},{64,66},{96,67},{4,68},{36,69},{68,70},{100,71},{8,... | collective-permute-start | bytes 393224 | tf_op jit(solution)/shard_map/ppermute | solution.py:108
  405.6 40.0 %collective-permute-start.54 = (f32[128,256]{1,0:T(8,128)}, f32[128,256]{1,0:T(8,128)}, u32[]{:S(2)}, u32[]{:S(2)}) collective-permute-start(f32[128,256]{1,0:T(8,128)} %get-tuple-element.50), channel_id=1, source_target_pairs={{0,96},{32,97},{64,98},{96,99},{4,100},{36,101},{68,102},{100,103}... | collective-permute-start | bytes 393224 | tf_op jit(solution)/shard_map/ppermute | solution.py:108
  444.5 32.3 %collective-permute-start.82 = (f32[256,256]{1,0:T(8,128)S(1)}, f32[256,256]{1,0:T(8,128)S(1)}, u32[]{:S(2)}, u32[]{:S(2)}) collective-permute-start(f32[256,256]{1,0:T(8,128)S(1)} %add.518), channel_id=1, source_target_pairs={{0,1},{1,0},{2,3},{3,2},{4,5},{5,4},{6,7},{7,6},{8,9},{9,8},{10,11... | collective-permute-start | bytes 786440 | tf_op jit(solution)/shard_map/ppermute | solution.py:38
  495.7 36.8 %collective-permute-start.83 = (f32[128,256]{1,0:T(8,128)S(1)}, f32[128,256]{1,0:T(8,128)S(1)}, u32[]{:S(2)}, u32[]{:S(2)}) collective-permute-start(f32[128,256]{1,0:T(8,128)S(1)} %slice_select_fusion.6), channel_id=1, source_target_pairs={{0,1},{1,0},{2,3},{3,2},{4,5},{5,4},{6,7},{7,6},{8,9},{9,8},{10,11... | collective-permute-start | bytes 393224 | tf_op jit(solution)/shard_map/ppermute | solution.py:38
  (100 other events, 1179.7 us)
Sparse Core Ops, SparseCore 0:
  53.4 106.8 all-gather.1
